TPU v7x, 128 devices: a whole 4x4x4 slice. The times are simulated.
128 devices in a mesh: row: 16 (over x_lo, y, core), col: 8 (over x_hi, z).
Axes of the slice: x: 4 (x_hi: 2, x_lo: 2; x = x_hi * 2 + x_lo), y: 4, z: 4, core: 2. Of those that a mesh axis runs over, the one named last changes fastest.
Arguments:
- nodes: bfloat16 [32768, 256], P(('row', 'col')), may hold values from -6 to 6
- weight: bfloat16 [256, 256], replicated, may hold values from -0.375 to 0.375
- adjacency: bfloat16 [32768, 32768], P('row', 'col'), may hold values from -0.046875 to 0.046875
- history: bfloat16 [131072, 256], P(('row', 'col')), may hold values from -6 to 6
- pull_owner: int32 [4096, 1], P(('row', 'col')), may hold values from 0 to 15; in each aligned block of 32 rows (0 to 31, 32 to 63, ...) at most 4 rows name the same one
- pull_slot: int32 [4096], P(('row', 'col')), may hold values from 0 to 7
- pull_target: int32 [4096], P(('row', 'col')), may hold values from 0 to 15
- hist_tiles: bfloat16 [4096, 128, 128], P(('row', 'col')), may hold values from -0.375 to 0.375
- cotangent: bfloat16 [32768, 256], P(('row', 'col')), may hold values from -6 to 6
Outputs:
- activated: bfloat16 [32768, 256], P(('row', 'col'))
- grad_nodes: bfloat16 [32768, 256], P(('row', 'col'))
- grad_weight: float32 [256, 256], replicated
Inputs may be any that keep to these rules, and one draw needn't show every extreme that they name: `pull_owner`: among the 32 pulls of one device no owner is named more than 4 times, a bound that some block reaches.
All inputs are finite; a program needn't handle non-finite values.
Results may differ from a plain program's by a relative error of at most 0.029.
Values may be sent and summed in bfloat16 or wider, within the bound.
A program may use at most 128 MiB of HBM per device.

v0:
```python
import math

import jax
import jax.numpy as jnp
from jax import lax
from jax.sharding import PartitionSpec as P

HID = 256
BLK = 128


def local(
    nodes, weight, adjacency, history, pull_owner, pull_slot, pull_target, hist_tiles, cotangent
):
    projected = jnp.dot(nodes, weight, preferred_element_type=jnp.float32).astype(jnp.bfloat16)
    gathered = lax.all_gather(projected, "row", axis=0, tiled=True)
    owners = pull_owner[:, 0]
    blocks = history.reshape(-1, BLK, HID)
    everything = lax.all_gather(blocks, "row", axis=0, tiled=True)
    pulled = everything[owners * blocks.shape[0] + pull_slot]
    products = jnp.einsum("kab,kbf->kaf", hist_tiles, pulled, preferred_element_type=jnp.float32)
    row_count = adjacency.shape[0] // BLK
    placing = (pull_target[None, :] == jnp.arange(row_count, dtype=jnp.int32)[:, None]).astype(
        jnp.float32
    )
    history_term = jnp.einsum(
        "jk,kaf->jaf", placing, products, precision=lax.Precision.HIGHEST
    ).reshape(-1, HID)
    in_batch = jnp.dot(adjacency, gathered, preferred_element_type=jnp.float32)
    mixed = lax.psum_scatter(
        (in_batch + history_term).astype(jnp.bfloat16), "col", scatter_dimension=0, tiled=True
    ).astype(jnp.float32)
    activated = jax.nn.silu(mixed).astype(jnp.bfloat16)
    sigmoid_z = jax.nn.sigmoid(mixed)
    grad_pre = (
        cotangent.astype(jnp.float32) * sigmoid_z * (1.0 + mixed * (1.0 - sigmoid_z))
    ).astype(jnp.bfloat16)
    grad_panel = lax.all_gather(grad_pre, "col", axis=0, tiled=True)
    grad_proj = lax.psum_scatter(
        lax.dot_general(
            adjacency, grad_panel, (((0,), (0,)), ((), ())), preferred_element_type=jnp.float32
        ).astype(jnp.bfloat16),
        "row",
        scatter_dimension=0,
        tiled=True,
    )
    grad_nodes = jnp.dot(grad_proj, weight.T, preferred_element_type=jnp.float32).astype(
        jnp.bfloat16
    )
    partial_grad = lax.dot_general(
        nodes, grad_proj, (((0,), (0,)), ((), ())), preferred_element_type=jnp.float32
    )
    all_nodes = nodes.shape[0] * lax.axis_size("row") * lax.axis_size("col")
    grad_weight = lax.psum(partial_grad, ("row", "col")) * (1.0 / math.sqrt(all_nodes))
    return (activated, grad_nodes, grad_weight)


def solution(mesh):
    return jax.shard_map(
        local,
        mesh=mesh,
        in_specs=(
            P(("row", "col"), None),
            P(),
            P("row", "col"),
            P(("row", "col"), None),
            P(("row", "col"), None),
            P(("row", "col")),
            P(("row", "col")),
            P(("row", "col"), None, None),
            P(("row", "col"), None),
        ),
        out_specs=(P(("row", "col"), None), P(("row", "col"), None), P()),
        check_vma=False,
    )
```

profile of v0, /device:TPU:1, one launch (start us, length us, event | category | flops | bytes accessed | tf_op | source)
XLA Modules:
  0.0 462.5 jit_solution(4636149198428322566)
XLA Ops:
  7.2 0.0 copy-start
  7.2 0.0 all-gather.6.cloned.1.call-start
  7.2 0.7 all-gather.6.cloned.1.call-update
  7.9 0.0 all-gather.4.cloned.1.call-start
  8.0 1.8 convolution_convert_fusion.2
  9.8 0.0 all-gather.4.cloned.1.call-update
  9.8 0.0 reduce-scatter.3.cloned.1.call-start
  9.8 0.7 compare_select_fusion
  10.5 54.9 %all-gather.6.cloned.1.call-done = bf16[128,128,256]{2,1,0:T(8,128)(2,1)} async-done(((bf16[8,128,256]{2,1,0:T(8,128)(2,1)}), bf16[128,128,256]{2,1,0:T(8,128)(2,1)}) %all-gather.6.cloned.1.call-update) | async-done | bytes 8388624 | tf_op jit(solution)/shard_map/all_gather | solution.py:19
  65.5 4.1 gather_fusion
  69.5 0.0 copy-done
  69.6 0.0 copy-start.4
  69.6 0.8 convolution_bitcast_fusion.1
  70.3 0.0 copy-done.4
  70.3 3.9 fusion.1
  74.3 28.5 %all-gather.4.cloned.1.call-done = bf16[4096,256]{1,0:T(8,128)(2,1)} async-done(((bf16[256,256]{1,0:T(8,128)(2,1)}), bf16[4096,256]{1,0:T(8,128)(2,1)}) %all-gather.4.cloned.1.call-update) | async-done | bytes 2097168 | tf_op jit(solution)/shard_map/all_gather | solution.py:16
  102.8 0.0 copy-start.3
  102.8 12.5 %fusion.4 = bf16[2048,256]{0,1:T(8,128)(2,1)} fusion(bf16[4096,256]{1,0:T(8,128)(2,1)} %all-gather.4.cloned.1.call-done, bf16[2048,4096]{1,0:T(8,128)(2,1)} %param.11, f32[32,8,16,128]{3,2,1,0:T(8,128)S(1)} %bitcast.38), kind=kOutput, calls=%fused_computation.7 | convolution fusion | flops 4296015872 | bytes 22020096 | tf_op jit(solution)/shard_map/dot_general | solution.py:29
  115.3 0.0 reduce-scatter.3.cloned.1.call-update
  115.3 0.0 all-gather.8.cloned.1.call-start
  115.3 0.0 copy-done.3
  115.4 0.1 copy.17
  115.5 69.4 %reduce-scatter.3.cloned.1.call-done = bf16[256,256]{0,1:T(8,128)(2,1)} async-done(((bf16[2048,256]{0,1:T(8,128)(2,1)}), bf16[256,256]{0,1:T(8,128)(2,1)}) %reduce-scatter.3.cloned.1.call-update) | async-done | bytes 131088 | tf_op jit(solution)/shard_map/reduce_scatter | solution.py:30
  184.9 1.7 fusion.11
  186.6 0.0 all-gather.8.cloned.1.call-update
  186.6 0.2 reduce-scatter.5.cloned.1.call-start
  186.8 46.5 %all-gather.8.cloned.1.call-done = bf16[2048,256]{0,1:T(8,128)(2,1)} async-done(((bf16[256,256]{0,1:T(8,128)(2,1)}), bf16[2048,256]{0,1:T(8,128)(2,1)}) %all-gather.8.cloned.1.call-update) | async-done | bytes 1048592 | tf_op jit(solution)/shard_map/all_gather | solution.py:38
  233.3 11.9 %fusion = bf16[4096,256]{0,1:T(8,128)(2,1)} fusion(bf16[2048,256]{0,1:T(8,128)(2,1)} %all-gather.8.cloned.1.call-done, bf16[2048,4096]{1,0:T(8,128)(2,1)} %param.11), kind=kOutput, calls=%fused_computation.2 | convolution fusion | flops 4296015872 | bytes 19922944 | tf_op jit(solution)/shard_map/dot_general | solution.py:40
  245.2 0.0 copy-start.2
  245.2 0.0 copy-start.1
  245.2 0.0 reduce-scatter.5.cloned.1.call-update
  245.3 0.0 all-reduce.2.cloned.1.call-start
  245.3 0.8 copy.18
  246.1 58.0 %reduce-scatter.5.cloned.1.call-done = bf16[256,256]{0,1:T(8,128)(2,1)} async-done(((bf16[4096,256]{0,1:T(8,128)(2,1)}), bf16[256,256]{0,1:T(8,128)(2,1)}) %reduce-scatter.5.cloned.1.call-update) | async-done | bytes 131088 | tf_op jit(solution)/shard_map/reduce_scatter | solution.py:39
  304.1 0.0 copy-done.2
  304.1 1.8 convolution_bitcast_fusion.2
  305.9 0.0 all-reduce.2.cloned.1.call-update
  305.9 0.0 copy-done.1
  305.9 1.8 convolution_convert_fusion.1
  307.7 146.1 %all-reduce.2.cloned.1.call-done = f32[256,256]{0,1:T(8,128)} async-done(((f32[256,256]{0,1:T(8,128)}), f32[256,256]{0,1:T(8,128)}) %all-reduce.2.cloned.1.call-update) | async-done | bytes 262160 | tf_op jit(solution)/shard_map/psum | solution.py:54
  453.8 1.0 broadcast_multiply_fusion
  454.8 0.8 copy.19
  (1 shorter events, 0.0 us)
Async XLA Ops:
  7.2 62.4 %copy-start = (bf16[32,128,128]{2,1,0:T(8,128)(2,1)S(1)}, bf16[32,128,128]{2,1,0:T(8,128)(2,1)}, u32[]{:S(2)}) copy-start(bf16[32,128,128]{2,1,0:T(8,128)(2,1)} %param.16) | copy-start | bytes 3145732
  7.2 58.3 %all-gather.6.cloned.1.call-start = ((), (), s32[]{:S(2)}) async-start(), calls=%async_computation.3 | async-start | bytes 8912896 | tf_op jit(solution)/shard_map/all_gather | solution.py:19
  7.9 94.9 %all-gather.4.cloned.1.call-start = ((), (), s32[]{:S(2)}) async-start(), calls=%async_computation.2 | async-start | bytes 2228224 | tf_op jit(solution)/shard_map/all_gather | solution.py:16
  9.8 175.1 %reduce-scatter.3.cloned.1.call-start = ((), (), s32[]{:S(2)}) async-start(), calls=%async_computation.4 | async-start | bytes 1179648 | tf_op jit(solution)/shard_map/reduce_scatter | solution.py:30
  69.6 0.8 copy-start.4
  102.8 12.6 %copy-start.3 = (bf16[256,256]{1,0:T(8,128)(2,1)S(1)}, bf16[256,256]{1,0:T(8,128)(2,1)}, u32[]{:S(2)}) copy-start(bf16[256,256]{1,0:T(8,128)(2,1)} %param.17) | copy-start | bytes 393220
  115.3 118.0 %all-gather.8.cloned.1.call-start = ((), (), s32[]{:S(2)}) async-start(), calls=%async_computation.5 | async-start | bytes 1179648 | tf_op jit(solution)/shard_map/all_gather | solution.py:38
  186.6 117.4 %reduce-scatter.5.cloned.1.call-start = ((), (), s32[]{:S(2)}) async-start(), calls=%async_computation.6 | async-start | bytes 2228224 | tf_op jit(solution)/shard_map/reduce_scatter | solution.py:39
  245.2 58.8 %copy-start.2 = (bf16[256,256]{1,0:T(8,128)(2,1)S(1)}, bf16[256,256]{1,0:T(8,128)(2,1)}, u32[]{:S(2)}) copy-start(bf16[256,256]{1,0:T(8,128)(2,1)} %param.9) | copy-start | bytes 393220
  245.2 60.6 %copy-start.1 = (bf16[256,256]{1,0:T(8,128)(2,1)S(1)}, bf16[256,256]{1,0:T(8,128)(2,1)}, u32[]{:S(2)}) copy-start(bf16[256,256]{1,0:T(8,128)(2,1)} %param.10) | copy-start | bytes 393220
  245.3 208.5 %all-reduce.2.cloned.1.call-start = ((), (), s32[]{:S(2)}) async-start(), calls=%async_computation.7 | async-start | bytes 524288 | tf_op jit(solution)/shard_map/psum | solution.py:54
Sparse Core Ops, SparseCore 0:
  9.7 55.7 all-gather.5
  67.7 34.9 all-gather.3
  115.4 69.4 reduce-scatter.2
  187.7 45.5 all-gather.7
  245.4 58.6 reduce-scatter.4
  310.0 143.8 all-reduce.1
where the time goes:
time: 463 us; the launch traced here: 462 us
  waiting for transfers between devices  404 us (87%)
  matrix products  34.5 us (7%)
  between operations  14.2 us (3%)
  local copies, waits for them, and re-layouts  5.78 us (1%)
    psum x1, waiting for transfers between devices, local(): lax.psum(partial_grad, ('row', 'col')) * (1.0 / math.sqrt(all_nodes))  146 us
    reduce_scatter x1, waiting for transfers between devices, local(): lax.psum_scatter((in_batch + history_term).astype(jnp.bfloat16), 'col', s...  69.4 us
    reduce_scatter x1, waiting for transfers between devices, local(): lax.psum_scatter(lax.dot_general(adjacency, grad_panel, (((0,), (0,)), ((...  58 us
    all_gather x1, waiting for transfers between devices, local(): everything = lax.all_gather(blocks, 'row', axis=0, tiled=True)  54.9 us
    all_gather x1, waiting for transfers between devices, local(): grad_panel = lax.all_gather(grad_pre, 'col', axis=0, tiled=True)  46.5 us
    all_gather x1, waiting for transfers between devices, local(): gathered = lax.all_gather(projected, 'row', axis=0, tiled=True)  28.5 us
    dot_general x1, matrix products, local(): in_batch = jnp.dot(adjacency, gathered, preferred_element_type=jnp.float32)  12.5 us
    dot_general x1, matrix products, local(): lax.dot_general(adjacency, grad_panel, (((0,), (0,)), ((), ())), preferre...  11.9 us
  transfers between devices with their start and end apart: 6, of which 6 were waited for; matrix products, arithmetic and copies ran while one was open for 3% of the time, Pallas kernels for 0%

commit v1 on v0

v1 whole, which is shorter than its diff:
```python
import math

import jax
import jax.numpy as jnp
from jax import lax
from jax.experimental import pallas as pl
from jax.experimental.pallas import tpu as pltpu
from jax.sharding import PartitionSpec as P

HID = 256
BLK = 128
HALF = 128
NR = 16
NC = 8
SPAN = 256
K = 32
MESH = pl.DeviceIdType.MESH
F32 = jnp.float32
BF16 = jnp.bfloat16


def kernel(
    chain_ref, owner_ref, slot_ref, nodes_hbm, w_hbm, adj_hbm, hist_hbm, tiles_hbm, cot_hbm,
    act_ref, gn_ref, gw_ref,
    nodes_all, hist0, hist1, adj, w, cot, tiles, proj, inb, sums,
    rs_snd, rs_rcv, gt, out_t, sib_snd, sib_rcv, d_snd, d_rcv,
    gwt, gw_rcv1, gw_sum, gw_rcv2, gw_all,
    loc_sem, snd_sem, ag_sem, rs_sem, g_sem, sib_sem, d_sem, gw1_sem, gw2_sem, gw3_sem,
):
    r = lax.axis_index("row")
    c = lax.axis_index("col")
    core = r % 2
    chip = r // 2
    x = chip // 4
    y = chip % 4
    other = 1 - x
    up = (y + 1) % 4
    down = (y + 3) % 4
    far = (y + 2) % 4
    sib = r + 1 - 2 * core

    def row_of(xx, yy, kk):
        return (xx * 4 + yy) * 2 + kk

    hist = (hist0, hist1)
    sent = []

    def send(src, dst, rsem, row, col):
        copy = pltpu.make_async_remote_copy(
            src_ref=src, dst_ref=dst, send_sem=snd_sem.at[len(sent)], recv_sem=rsem,
            device_id=(row, col), device_id_type=MESH,
        )
        copy.start()
        sent.append(copy)

    def arrive(dst, rsem):
        pltpu.make_async_remote_copy(
            src_ref=dst, dst_ref=dst, send_sem=snd_sem.at[0], recv_sem=rsem,
            device_id=(sib, c), device_id_type=MESH,
        ).wait_recv()

    def local(src, dst, i):
        copy = pltpu.make_async_copy(src, dst, loc_sem.at[i])
        copy.start()
        return copy

    own_nodes = local(nodes_hbm, nodes_all.at[r], 0)
    own_hist = [
        local(hist_hbm.at[:, :, pl.ds(h * HALF, HALF)], hist[h].at[pl.ds(r * 8, 8)], 1 + h)
        for h in range(2)
    ]
    w_copy = local(w_hbm, w, 3)
    adj_copy = local(adj_hbm, adj, 4)
    tiles_copy = local(tiles_hbm, tiles, 5)
    cot_copy = local(cot_hbm, cot, 6)

    barrier = pltpu.get_barrier_semaphore()
    for d in range(1, NR):
        pl.semaphore_signal(barrier, inc=1, device_id=((r + d) % NR, c), device_id_type=MESH)
    for d in range(1, NC):
        pl.semaphore_signal(barrier, inc=1, device_id=(r, (c + d) % NC), device_id_type=MESH)
    pl.semaphore_wait(barrier, NR + NC - 2)

    def piece(chunk, owner, part):
        if chunk == 0:
            ref = nodes_all.at[owner]
            return ref if part is None else ref.at[pl.ds(part * 128, 128)]
        if part is None:
            return hist[chunk - 1].at[pl.ds(owner * 8, 8)]
        return hist[chunk - 1].at[pl.ds(owner * 8 + part * 4, 4)]

    def push(chunk, owner, part, dest):
        ref = piece(chunk, owner, part)
        send(ref, ref, ag_sem.at[chunk, owner, part or 0], dest, c)

    def got(chunk, owner, part=None):
        arrive(piece(chunk, owner, part), ag_sem.at[chunk, owner, part or 0])

    def own_sends(chunk):
        push(chunk, r, None, row_of(other, y, core))
        push(chunk, r, None, row_of(x, up, core))
        push(chunk, r, None, row_of(x, down, core))
        push(chunk, r, None, sib)

    def step_a(chunk):
        o = row_of(other, y, core)
        got(chunk, o)
        push(chunk, o, None, row_of(x, up, core))
        push(chunk, o, None, row_of(x, down, core))
        push(chunk, o, None, sib)

    def step_b(chunk):
        o = row_of(x, down, core)
        got(chunk, o)
        push(chunk, o, 0, row_of(x, up, core))
        push(chunk, o, None, sib)
        o = row_of(x, up, core)
        got(chunk, o)
        push(chunk, o, 1, row_of(x, down, core))
        push(chunk, o, None, sib)

    def step_c(chunk):
        for yy in (down, up):
            o = row_of(other, yy, core)
            got(chunk, o)
            push(chunk, o, None, sib)

    def step_d(chunk):
        o = row_of(x, far, core)
        for part in range(2):
            got(chunk, o, part)
            push(chunk, o, part, row_of(other, y, core))
            push(chunk, o, part, sib)

    def step_e(chunk):
        o = row_of(other, far, core)
        for part in range(2):
            got(chunk, o, part)
            push(chunk, o, part, sib)

    def step_f(chunk):
        k = 1 - core
        for xx, yy in ((x, y), (other, y), (x, down), (x, up), (other, down), (other, up)):
            got(chunk, row_of(xx, yy, k))
        for xx in (x, other):
            for part in range(2):
                got(chunk, row_of(xx, far, k), part)

    def forward_piece(i):
        rows = pl.ds(i * 512, 512)
        v = jnp.dot(adj[rows, :], proj[...], preferred_element_type=F32)
        inb[0, rows, :] = v[:, :HALF]
        inb[1, rows, :] = v[:, HALF:]

    def history_and_scatter(h):
        sums[0] = jnp.zeros((BLK, HALF), F32)

        def pull(k, carry):
            block = hist[h][owner_ref[k] * 8 + slot_ref[k]]
            term = jnp.dot(tiles[k], block, preferred_element_type=F32)
            sums[k + 1] = term + sums[chain_ref[k]]
            return carry

        lax.fori_loop(0, K, pull, 0)

        def place(j, carry):
            v = inb[h, pl.ds(pl.multiple_of(j * BLK, BLK), BLK), :] + sums[chain_ref[K + j]]
            rs_snd[h, j // 2, pl.ds(pl.multiple_of((j % 2) * BLK, BLK), BLK), :] = v.astype(BF16)
            return carry

        lax.fori_loop(0, 2 * NC, place, 0)
        for d in range(1, NC):
            cc = (c + d) % NC
            send(rs_snd.at[h, cc], rs_rcv.at[h, c], rs_sem.at[h, c], r, cc)

    def activate(h):
        cols = pl.ds(h * HALF, HALF)
        mixed = rs_snd[h, c].astype(F32)
        for d in range(1, NC):
            cc = (c + d) % NC
            arrive(rs_rcv.at[h, cc], rs_sem.at[h, cc])
            mixed = mixed + rs_rcv[h, cc].astype(F32)
        s = 1.0 / (1.0 + jnp.exp(-mixed))
        act_ref[:, cols] = (mixed * s).astype(BF16)
        g = cot[:, cols].astype(F32) * s * (1.0 + mixed * (1.0 - s))
        gt[h, c] = g.T.astype(BF16)
        for d in range(1, NC):
            send(gt.at[h, c], gt.at[h, c], g_sem.at[h, c], r, (c + d) % NC)

    def backward(h):
        for d in range(NC):
            cc = (c + d) % NC
            if d:
                arrive(gt.at[h, cc], g_sem.at[h, cc])
            rows = pl.ds(pl.multiple_of(cc * SPAN, SPAN), SPAN)
            lhs = gt[h, cc]

            def tile(n, carry, rows=rows, lhs=lhs, d=d):
                cols = pl.ds(pl.multiple_of(n * 512, 512), 512)
                v = jnp.dot(lhs, adj[rows, cols], preferred_element_type=F32)
                out_t[:, cols] = v if d == 0 else out_t[:, cols] + v
                return carry

            lax.fori_loop(0, 8, tile, 0)

        def for_sib(q, carry):
            cols = pl.ds(pl.multiple_of((2 * q + 1 - core) * SPAN, SPAN), SPAN)
            sib_snd[h, q] = out_t[:, cols].astype(BF16)
            return carry

        lax.fori_loop(0, 8, for_sib, 0)
        send(sib_snd.at[h], sib_rcv.at[h], sib_sem.at[h], sib, c)

        def weight_term(o, total):
            cols = pl.ds(pl.multiple_of(o * SPAN, SPAN), SPAN)
            return total + jnp.dot(
                out_t[:, cols].astype(BF16), nodes_all[o], preferred_element_type=F32
            )

        gwt[pl.ds(h * HALF, HALF), :] = lax.fori_loop(
            0, NR, weight_term, jnp.zeros((HALF, HID), F32)
        )

    def scatter_rows(h):
        arrive(sib_rcv.at[h], sib_sem.at[h])

        def add(q, carry):
            cols = pl.ds(pl.multiple_of((2 * q + core) * SPAN, SPAN), SPAN)
            d_snd[h, q] = (out_t[:, cols] + sib_rcv[h, q].astype(F32)).astype(BF16)
            return carry

        lax.fori_loop(0, 8, add, 0)
        for d in range(1, 8):
            qq = (chip + d) % 8
            send(d_snd.at[h, qq], d_rcv.at[h, chip], d_sem.at[h, chip], qq * 2 + core, c)

    def collect_rows(h):
        total = d_snd[h, chip].astype(F32)
        for d in range(1, 8):
            qq = (chip + d) % 8
            arrive(d_rcv.at[h, qq], d_sem.at[h, qq])
            total = total + d_rcv[h, qq].astype(F32)
        return lax.dot_general(
            total.T.astype(BF16), w[:, pl.ds(h * HALF, HALF)], (((1,), (1,)), ((), ())),
            preferred_element_type=F32,
        )

    own_nodes.wait()
    own_sends(0)
    own_hist[0].wait()
    own_sends(1)
    own_hist[1].wait()
    for step in (step_a, step_b, step_c, step_d, step_e, step_f):
        step(0)
    step_a(1)
    w_copy.wait()

    def project(o, carry):
        rows = pl.ds(pl.multiple_of(o * SPAN, SPAN), SPAN)
        proj[rows, :] = jnp.dot(nodes_all[o], w[...], preferred_element_type=F32).astype(BF16)
        return carry

    lax.fori_loop(0, NR, project, 0)
    step_b(1)
    own_sends(2)
    adj_copy.wait()
    forward_piece(0)
    forward_piece(1)
    step_c(1)
    forward_piece(2)
    step_d(1)
    forward_piece(3)
    step_a(2)
    step_e(1)
    tiles_copy.wait()
    cot_copy.wait()
    step_f(1)
    history_and_scatter(0)
    for step in (step_b, step_c, step_d, step_e):
        step(2)
    activate(0)
    step_f(2)
    history_and_scatter(1)
    backward(0)
    scatter_rows(0)
    activate(1)
    backward(1)
    for d in range(1, NR):
        rr = (r + d) % NR
        send(
            gwt.at[pl.ds(pl.multiple_of(rr * 16, 16), 16)], gw_rcv1.at[r], gw1_sem.at[r], rr, c
        )
    scatter_rows(1)
    part = collect_rows(0)
    total = gwt[pl.ds(pl.multiple_of(r * 16, 16), 16), :]
    for d in range(1, NR):
        rr = (r + d) % NR
        arrive(gw_rcv1.at[rr], gw1_sem.at[rr])
        total = total + gw_rcv1[rr]
    gw_rcv2[c] = total
    for d in range(1, NC):
        send(gw_rcv2.at[c], gw_rcv2.at[c], gw2_sem.at[c], r, (c + d) % NC)
    for d in range(1, NC):
        cc = (c + d) % NC
        arrive(gw_rcv2.at[cc], gw2_sem.at[cc])
    total = gw_rcv2[0]
    for i in range(1, NC):
        total = total + gw_rcv2[i]
    gw_all[r] = total
    for d in range(1, NR):
        send(gw_all.at[r], gw_all.at[r], gw3_sem.at[r], (r + d) % NR, c)
    gn_ref[...] = (part + collect_rows(1)).astype(BF16)
    for d in range(1, NR):
        rr = (r + d) % NR
        arrive(gw_all.at[rr], gw3_sem.at[rr])
    gw_ref[...] = gw_all[...]
    for copy in sent:
        copy.wait_send()


def local(
    nodes, weight, adjacency, history, pull_owner, pull_slot, pull_target, hist_tiles, cotangent
):
    ask = jnp.concatenate([pull_target, jnp.arange(2 * NC, dtype=jnp.int32)])
    limit = jnp.minimum(jnp.arange(K + 2 * NC, dtype=jnp.int32), K)
    pulls = jnp.arange(K, dtype=jnp.int32)
    match = (pull_target[None, :] == ask[:, None]) & (pulls[None, :] < limit[:, None])
    chain = jnp.max(jnp.where(match, pulls[None, :] + 1, 0), axis=1)
    smem = pl.BlockSpec(memory_space=pltpu.SMEM)
    any_ = pl.BlockSpec(memory_space=pl.ANY)
    vmem = pl.BlockSpec(memory_space=pltpu.VMEM)
    dma = pltpu.SemaphoreType.DMA
    act, grad_nodes, gw = pl.pallas_call(
        kernel,
        out_shape=(
            jax.ShapeDtypeStruct((SPAN, HID), BF16),
            jax.ShapeDtypeStruct((SPAN, HID), BF16),
            jax.ShapeDtypeStruct((NR, 16, HID), F32),
        ),
        in_specs=[smem] * 3 + [any_] * 6,
        out_specs=(vmem,) * 3,
        scratch_shapes=[
            pltpu.VMEM((NR, SPAN, HID), BF16),
            pltpu.VMEM((128, BLK, HALF), BF16),
            pltpu.VMEM((128, BLK, HALF), BF16),
            pltpu.VMEM((2048, 4096), BF16),
            pltpu.VMEM((HID, HID), BF16),
            pltpu.VMEM((SPAN, HID), BF16),
            pltpu.VMEM((K, BLK, BLK), BF16),
            pltpu.VMEM((4096, HID), BF16),
            pltpu.VMEM((2, 2048, HALF), F32),
            pltpu.VMEM((K + 1, BLK, HALF), F32),
            pltpu.VMEM((2, NC, SPAN, HALF), BF16),
            pltpu.VMEM((2, NC, SPAN, HALF), BF16),
            pltpu.VMEM((2, NC, HALF, SPAN), BF16),
            pltpu.VMEM((HALF, 4096), F32),
            pltpu.VMEM((2, 8, HALF, SPAN), BF16),
            pltpu.VMEM((2, 8, HALF, SPAN), BF16),
            pltpu.VMEM((2, 8, HALF, SPAN), BF16),
            pltpu.VMEM((2, 8, HALF, SPAN), BF16),
            pltpu.VMEM((HID, HID), F32),
            pltpu.VMEM((NR, 16, HID), F32),
            pltpu.VMEM((16, HID), F32),
            pltpu.VMEM((NC, 16, HID), F32),
            pltpu.VMEM((NR, 16, HID), F32),
            dma((8,)),
            dma((160,)),
            dma((3, NR, 2)),
            dma((2, NC)),
            dma((2, NC)),
            dma((2,)),
            dma((2, 8)),
            dma((NR,)),
            dma((NC,)),
            dma((NR,)),
        ],
        compiler_params=pltpu.CompilerParams(
            collective_id=0, has_side_effects=True, vmem_limit_bytes=60 * 2**20
        ),
    )(
        chain, pull_owner[:, 0], pull_slot, nodes, weight, adjacency,
        history.reshape(8, BLK, HID), hist_tiles, cotangent,
    )
    all_nodes = nodes.shape[0] * NR * NC
    grad_weight = gw.reshape(HID, HID).T * (1.0 / math.sqrt(all_nodes))
    return act, grad_nodes, grad_weight


def solution(mesh):
    return jax.shard_map(
        local,
        mesh=mesh,
        in_specs=(
            P(("row", "col"), None),
            P(),
            P("row", "col"),
            P(("row", "col"), None),
            P(("row", "col"), None),
            P(("row", "col")),
            P(("row", "col")),
            P(("row", "col"), None, None),
            P(("row", "col"), None),
        ),
        out_specs=(P(("row", "col"), None), P(("row", "col"), None), P()),
        check_vma=False,
    )
```

time: 463 us -> 146 us (0.32)
  waiting for transfers between devices: 404 us -> 0 us
  Pallas kernels: 0 us -> 138 us
  matrix products: 34.5 us -> 0 us
  between operations: 14.2 us -> 0.66 us
    psum x1 -> x0, waiting for transfers between devices: 146 us -> none  [local(): lax.psum(partial_grad, ('row', 'col')) * (1.0 / math.sqrt(all_nodes))]
    pallas_call x0 -> x1, Pallas kernels: none -> 138 us  [local(): pl.pallas_call(kernel, out_shape=(jax.ShapeDtypeStruct((SPAN, HID), BF16)...]
    all_gather x3 -> x0, waiting for transfers between devices: 130 us -> none  [the longest x1 54.9 us: local(): everything = lax.all_gather(blocks, 'row', axis=0, tiled=True)]
    reduce_scatter x2 -> x0, waiting for transfers between devices: 127 us -> none  [the longest x1 69.4 us: local(): lax.psum_scatter((in_batch + history_term).astype(jnp.bfloat16), 'col', s...]
    dot_general x7 -> x0, matrix products: 34.5 us -> none  [the longest x1 12.5 us: local(): in_batch = jnp.dot(adjacency, gathered, preferred_element_type=jnp.float32)]
  transfers between devices with their start and end apart: 6 -> 0, of which waited for: 6 -> 0; matrix products, arithmetic and copies ran while one was open for 3% -> 0% of each run, Pallas kernels for 0% -> 0%
where the time goes in v1:
time: 146 us
  Pallas kernels  138 us (95%)
  local copies, waits for them, and re-layouts  3.97 us (3%)
  other arithmetic  2.97 us (2%)
    pallas_call x1, Pallas kernels, local(): pl.pallas_call(kernel, out_shape=(jax.ShapeDtypeStruct((SPAN, HID), BF16)...  138 us
    unnamed x2, local copies, waits for them, and re-layouts  3.13 us

profile of v1, /device:TPU:1, one launch (start us, length us, event | category | flops | bytes accessed | tf_op | source)
XLA Modules:
  0.0 145.7 jit_solution(7758109106810476110)
XLA Ops:
  0.6 0.7 pad_add_fusion
  1.4 1.3 select_reduce_fusion.chain_ref
  2.6 138.1 %shard_map.112 = (bf16[256,256]{1,0:T(8,128)(2,1)}, bf16[256,256]{1,0:T(8,128)(2,1)}, f32[16,16,256]{2,1,0:T(8,128)}) custom-call(s32[48]{0:T(128)} %select_reduce_fusion.chain_ref, s32[32]{0:T(128)} %bitcast.7, s32[32]{0:T(128)} %slot_ref.1, bf16[256,256]{1,0:T(8,128)(2,1)} %nodes_hbm.1, bf16[256,256]{1,0:T(8,128)(2,1)} %w_hbm.1, ...), custom_call_target="tpu_custom_call" | custom-call | tf_op jit(solution)/shard_map/pallas_call | solution.py:333
  140.8 1.0 broadcast_multiply_fusion
  141.8 0.8 copy.13
  142.6 1.6 %copy.16 = bf16[256,256]{1,0:T(8,128)(2,1)} copy(bf16[256,256]{1,0:T(8,128)(2,1)} %get-tuple-element.14) | data formatting | bytes 262144
  144.2 1.6 %copy.17 = bf16[256,256]{1,0:T(8,128)(2,1)} copy(bf16[256,256]{1,0:T(8,128)(2,1)} %get-tuple-element.15) | data formatting | bytes 262144
  (2 shorter events, 0.0 us)

commit v2 on v1

v2 whole, which is shorter than its diff:
```python
import math

import jax
import jax.numpy as jnp
from jax import lax
from jax.experimental import pallas as pl
from jax.experimental.pallas import tpu as pltpu
from jax.sharding import PartitionSpec as P

HID = 256
BLK = 128
HALF = 128
NR = 16
NC = 8
SPAN = 256
K = 32
MESH = pl.DeviceIdType.MESH
F32 = jnp.float32
BF16 = jnp.bfloat16


def kernel(
    owner_ref, slot_ref, target_ref, nodes_hbm, w_hbm, adj_hbm, hist_hbm, tiles_hbm, cot_hbm,
    act_ref, gn_ref, gw_ref,
    nodes_all, hist0, hist1, adj, w, cot, tiles, mix, inb, sums,
    rs_snd, rs_rcv, gt, sib_snd, sib_rcv, d_snd, d_rcv,
    gwt, gw_rcv1, gw_rcv2, gw_all, chain_v, chain_ref,
    loc_sem, snd_sem, ag_sem, rs_sem, g_sem, sib_snd_sem, sib_sem, d_snd_sem, d_sem,
    gw1_sem, gw2_sem, gw3_sem, near_sem, far_sem,
):
    r = lax.axis_index("row")
    c = lax.axis_index("col")
    core = r % 2
    chip = r // 2
    x = chip // 4
    y = chip % 4
    other = 1 - x
    up = (y + 1) % 4
    down = (y + 3) % 4
    far = (y + 2) % 4
    sib = r + 1 - 2 * core
    z = c % 4
    z_up = c - z + (z + 1) % 4
    z_down = c - z + (z + 3) % 4
    c_across = (c + 4) % NC

    def row_of(xx, yy, kk):
        return (xx * 4 + yy) * 2 + kk

    hist = (hist0, hist1)
    sent = []

    def send(src, dst, rsem, row, col):
        copy = pltpu.make_async_remote_copy(
            src_ref=src, dst_ref=dst, send_sem=snd_sem.at[len(sent)], recv_sem=rsem,
            device_id=(row, col), device_id_type=MESH,
        )
        copy.start()
        sent.append(copy)

    def arrive(dst, rsem):
        pltpu.make_async_remote_copy(
            src_ref=dst, dst_ref=dst, send_sem=snd_sem.at[0], recv_sem=rsem,
            device_id=(sib, c), device_id_type=MESH,
        ).wait_recv()

    def local(src, dst, i):
        copy = pltpu.make_async_copy(src, dst, loc_sem.at[i])
        copy.start()
        return copy

    def span(i):
        return pl.ds(pl.multiple_of(i * SPAN, SPAN), SPAN)

    own_nodes = local(nodes_hbm, nodes_all.at[span(r)], 0)
    own_hist = [
        local(hist_hbm.at[:, :, pl.ds(h * HALF, HALF)], hist[h].at[pl.ds(r * 8, 8)], 1 + h)
        for h in range(2)
    ]
    w_copy = local(w_hbm, w, 3)
    adj_copy = local(adj_hbm, adj, 4)
    tiles_copy = local(tiles_hbm, tiles, 5)
    cot_copy = local(cot_hbm, cot, 6)

    barrier = pltpu.get_barrier_semaphore()
    for rr, cc in (
        (row_of(other, y, core), c), (row_of(x, up, core), c), (row_of(x, down, core), c), (sib, c),
        (r, z_up), (r, z_down), (r, c_across),
    ):
        pl.semaphore_signal(barrier, inc=1, device_id=(rr, cc), device_id_type=MESH)
    pl.semaphore_wait(barrier, 7)

    def piece(chunk, owner, part):
        if chunk == 0:
            if part is None:
                return nodes_all.at[span(owner)]
            return nodes_all.at[pl.ds(pl.multiple_of(owner * SPAN + part * 128, 128), 128)]
        if part is None:
            return hist[chunk - 1].at[pl.ds(owner * 8, 8)]
        return hist[chunk - 1].at[pl.ds(owner * 8 + part * 4, 4)]

    def push(chunk, owner, part, dest):
        ref = piece(chunk, owner, part)
        send(ref, ref, ag_sem.at[chunk, owner, part or 0], dest, c)

    def got(chunk, owner, part=None):
        arrive(piece(chunk, owner, part), ag_sem.at[chunk, owner, part or 0])

    def own_y(chunk):
        push(chunk, r, None, row_of(x, up, core))
        push(chunk, r, None, row_of(x, down, core))

    def own_x(chunk):
        push(chunk, r, None, row_of(other, y, core))
        push(chunk, r, None, sib)

    def step_a(chunk):
        o = row_of(other, y, core)
        got(chunk, o)
        push(chunk, o, None, row_of(x, up, core))
        push(chunk, o, None, row_of(x, down, core))
        push(chunk, o, None, sib)

    def step_b(chunk):
        o = row_of(x, down, core)
        got(chunk, o)
        push(chunk, o, 0, row_of(x, up, core))
        push(chunk, o, None, sib)
        o = row_of(x, up, core)
        got(chunk, o)
        push(chunk, o, 1, row_of(x, down, core))
        push(chunk, o, None, sib)

    def step_c(chunk):
        for yy in (down, up):
            o = row_of(other, yy, core)
            got(chunk, o)
            push(chunk, o, None, sib)

    def step_d(chunk):
        o = row_of(x, far, core)
        for part in range(2):
            got(chunk, o, part)
            push(chunk, o, part, row_of(other, y, core))
            push(chunk, o, part, sib)

    def step_e(chunk):
        o = row_of(other, far, core)
        for part in range(2):
            got(chunk, o, part)
            push(chunk, o, part, sib)

    def step_f(chunk):
        k = 1 - core
        for xx, yy in ((x, y), (other, y), (x, down), (x, up), (other, down), (other, up)):
            got(chunk, row_of(xx, yy, k))
        for xx in (x, other):
            for part in range(2):
                got(chunk, row_of(xx, far, k), part)

    def make_chain():
        lane = lax.broadcasted_iota(jnp.int32, (K, 128), 1)
        sub = lax.broadcasted_iota(jnp.int32, (K, 128), 0)
        ask, mine = lane - K, sub
        for k in range(K):
            t = target_ref[k]
            ask = jnp.where(lane == k, t, ask)
            mine = jnp.where(sub == k, t, mine)
        match = (mine == ask) & (sub < jnp.minimum(lane, K))
        chain_v[...] = jnp.max(jnp.where(match, sub + 1, 0), axis=0, keepdims=True)
        return local(chain_v, chain_ref, 7)

    def forward_piece(i):
        rows = pl.ds(i * 512, 512)
        m = jnp.dot(adj[rows, :], nodes_all[...], preferred_element_type=F32).astype(BF16)
        mix[rows, :] = m
        v = jnp.dot(m, w[...], preferred_element_type=F32)
        inb[0, rows, :] = v[:, :HALF]
        inb[1, rows, :] = v[:, HALF:]

    def history_and_scatter(h):
        sums[0] = jnp.zeros((BLK, HALF), F32)

        def product(k, carry):
            block = hist[h][owner_ref[k] * 8 + slot_ref[k]]
            sums[k + 1] = jnp.dot(tiles[k], block, preferred_element_type=F32)
            return carry

        lax.fori_loop(0, K, product, 0, unroll=8)

        def link(k, carry):
            sums[k + 1] = sums[k + 1] + sums[chain_ref[0, k]]
            return carry

        lax.fori_loop(0, K, link, 0, unroll=4)
        for d in range(1, NC + 1):
            cc = (c + d) % NC
            for i in range(2):
                j = cc * 2 + i
                v = inb[h, pl.ds(pl.multiple_of(j * BLK, BLK), BLK), :] + sums[chain_ref[0, K + j]]
                rs_snd[h, cc, pl.ds(i * BLK, BLK), :] = v.astype(BF16)
            if d < NC:
                send(rs_snd.at[h, cc], rs_rcv.at[h, c], rs_sem.at[h, c], r, cc)

    def activate(h):
        cols = pl.ds(h * HALF, HALF)
        mixed = rs_snd[h, c].astype(F32)
        for d in range(1, NC):
            cc = (c + NC - d) % NC
            arrive(rs_rcv.at[h, cc], rs_sem.at[h, cc])
            mixed = mixed + rs_rcv[h, cc].astype(F32)
        s = 1.0 / (1.0 + jnp.exp(-mixed))
        g = cot[:, cols].astype(F32) * s * (1.0 + mixed * (1.0 - s))
        own = gt.at[h, :, span(c)]
        own[...] = g.T.astype(BF16)
        for d in range(1, NC):
            send(own, own, g_sem.at[h, c], r, (c + d) % NC)
        act_ref[:, cols] = (mixed * s).astype(BF16)

    def sib_copy(h, q):
        return pltpu.make_async_remote_copy(
            src_ref=sib_snd.at[h, q], dst_ref=sib_rcv.at[h, q], send_sem=sib_snd_sem.at[h, q],
            recv_sem=sib_sem.at[h, q], device_id=(sib, c), device_id_type=MESH,
        )

    def row_copy(h, q):
        return pltpu.make_async_remote_copy(
            src_ref=d_snd.at[h, q], dst_ref=d_rcv.at[h, chip], send_sem=d_snd_sem.at[h, q],
            recv_sem=d_sem.at[h, chip], device_id=(q * 2 + core, c), device_id_type=MESH,
        )

    def backward(h):
        for d in range(1, NC):
            cc = (c + NC - d) % NC
            arrive(gt.at[h, :, span(cc)], g_sem.at[h, cc])
        gwt[pl.ds(h * HALF, HALF), :] = jnp.dot(gt[h], mix[...], preferred_element_type=F32)
        if h:
            for d in range(1, NR):
                rr = (r + d) % NR
                rows = pl.ds(pl.multiple_of(rr * 16, 16), 16)
                send(gwt.at[rows], gw_rcv1.at[r], gw1_sem.at[r], rr, c)

        def for_sib(d, carry):
            q = (chip + d) % 8
            v = jnp.dot(gt[h], adj[:, span(2 * q + 1 - core)], preferred_element_type=F32)
            sib_snd[h, q] = v.astype(BF16)
            sib_copy(h, q).start()
            return carry

        lax.fori_loop(1, 9, for_sib, 0)

        def summed(q):
            v = jnp.dot(gt[h], adj[:, span(2 * q + core)], preferred_element_type=F32)
            arrive(sib_rcv.at[h, q], sib_sem.at[h, q])
            d_snd[h, q] = (v + sib_rcv[h, q].astype(F32)).astype(BF16)

        def for_chip(d, carry):
            q = (chip + d) % 8
            summed(q)
            row_copy(h, q).start()
            return carry

        lax.fori_loop(1, 8, for_chip, 0)
        summed(chip)

    def collect_rows(h):
        total = d_snd[h, chip].astype(F32)
        for d in range(1, 8):
            qq = (chip + 8 - d) % 8
            arrive(d_rcv.at[h, qq], d_sem.at[h, qq])
            total = total + d_rcv[h, qq].astype(F32)
        return lax.dot_general(
            total.T.astype(BF16), w[:, pl.ds(h * HALF, HALF)], (((1,), (1,)), ((), ())),
            preferred_element_type=F32,
        )

    own_nodes.wait()
    own_y(0)
    own_x(0)
    own_hist[0].wait()
    own_y(1)
    own_x(1)
    for cc in (z_up, z_down):
        pl.semaphore_signal(near_sem, inc=1, device_id=(r, cc), device_id_type=MESH)
    own_hist[1].wait()
    chain_copy = make_chain()
    step_b(0)
    step_a(0)
    own_x(2)
    pl.semaphore_wait(near_sem, 2)
    pl.semaphore_signal(far_sem, inc=1, device_id=(r, c_across), device_id_type=MESH)
    step_c(0)
    step_d(0)
    step_b(1)
    own_y(2)
    step_a(1)
    step_e(0)
    step_f(0)
    w_copy.wait()
    adj_copy.wait()
    forward_piece(0)
    forward_piece(1)
    step_d(1)
    forward_piece(2)
    forward_piece(3)
    step_b(2)
    step_a(2)
    step_e(1)
    step_c(1)
    tiles_copy.wait()
    cot_copy.wait()
    chain_copy.wait()
    pl.semaphore_wait(far_sem, 1)
    step_f(1)
    history_and_scatter(0)
    step_d(2)
    step_c(2)
    activate(0)
    step_e(2)
    step_f(2)
    history_and_scatter(1)
    backward(0)
    activate(1)
    part = collect_rows(0)
    backward(1)
    total = gwt[pl.ds(pl.multiple_of(r * 16, 16), 16), :]
    for d in range(1, NR):
        rr = (r + NR - d) % NR
        arrive(gw_rcv1.at[rr], gw1_sem.at[rr])
        total = total + gw_rcv1[rr]
    gw_rcv2[c] = total
    for d in range(1, NC):
        send(gw_rcv2.at[c], gw_rcv2.at[c], gw2_sem.at[c], r, (c + d) % NC)
    for d in range(1, NC):
        cc = (c + NC - d) % NC
        arrive(gw_rcv2.at[cc], gw2_sem.at[cc])
    total = gw_rcv2[0]
    for i in range(1, NC):
        total = total + gw_rcv2[i]
    gw_all[r] = total
    for d in range(1, NR):
        send(gw_all.at[r], gw_all.at[r], gw3_sem.at[r], (r + d) % NR, c)
    gn_ref[...] = (part + collect_rows(1)).astype(BF16)
    for d in range(1, NR):
        rr = (r + NR - d) % NR
        arrive(gw_all.at[rr], gw3_sem.at[rr])
    gw_ref[...] = gw_all[...]
    for copy in sent:
        copy.wait_send()

    def sent_tiles(d, carry):
        q = (chip + d) % 8
        for h in range(2):
            sib_copy(h, q).wait_send()
            row_copy(h, q).wait_send()
        return carry

    lax.fori_loop(1, 8, sent_tiles, 0)
    for h in range(2):
        sib_copy(h, chip).wait_send()


def finish(scale, act_ref, gn_ref, gw_ref, act_out, gn_out, gw_out, sem):
    copies = [
        pltpu.make_async_copy(act_ref, act_out, sem.at[0]),
        pltpu.make_async_copy(gn_ref, gn_out, sem.at[1]),
    ]
    for copy in copies:
        copy.start()
    gw_out[...] = gw_ref[...].T * scale
    for copy in copies:
        copy.wait()


def local(
    nodes, weight, adjacency, history, pull_owner, pull_slot, pull_target, hist_tiles, cotangent
):
    smem = pl.BlockSpec(memory_space=pltpu.SMEM)
    any_ = pl.BlockSpec(memory_space=pl.ANY)
    vmem = pl.BlockSpec(memory_space=pltpu.VMEM)
    dma = pltpu.SemaphoreType.DMA
    act, grad_nodes, gw = pl.pallas_call(
        kernel,
        out_shape=(
            jax.ShapeDtypeStruct((SPAN, HID), BF16),
            jax.ShapeDtypeStruct((SPAN, HID), BF16),
            jax.ShapeDtypeStruct((NR, 16, HID), F32),
        ),
        in_specs=[smem] * 3 + [any_] * 6,
        out_specs=(vmem,) * 3,
        scratch_shapes=[
            pltpu.VMEM((4096, HID), BF16),
            pltpu.VMEM((128, BLK, HALF), BF16),
            pltpu.VMEM((128, BLK, HALF), BF16),
            pltpu.VMEM((2048, 4096), BF16),
            pltpu.VMEM((HID, HID), BF16),
            pltpu.VMEM((SPAN, HID), BF16),
            pltpu.VMEM((K, BLK, BLK), BF16),
            pltpu.VMEM((2048, HID), BF16),
            pltpu.VMEM((2, 2048, HALF), F32),
            pltpu.VMEM((K + 1, BLK, HALF), F32),
            pltpu.VMEM((2, NC, SPAN, HALF), BF16),
            pltpu.VMEM((2, NC, SPAN, HALF), BF16),
            pltpu.VMEM((2, HALF, 2048), BF16),
            pltpu.VMEM((2, 8, HALF, SPAN), BF16),
            pltpu.VMEM((2, 8, HALF, SPAN), BF16),
            pltpu.VMEM((2, 8, HALF, SPAN), BF16),
            pltpu.VMEM((2, 8, HALF, SPAN), BF16),
            pltpu.VMEM((HID, HID), F32),
            pltpu.VMEM((NR, 16, HID), F32),
            pltpu.VMEM((NC, 16, HID), F32),
            pltpu.VMEM((NR, 16, HID), F32),
            pltpu.VMEM((1, 128), jnp.int32),
            pltpu.SMEM((1, 128), jnp.int32),
            dma((8,)),
            dma((160,)),
            dma((3, NR, 2)),
            dma((2, NC)),
            dma((2, NC)),
            dma((2, 8)),
            dma((2, 8)),
            dma((2, 8)),
            dma((2, 8)),
            dma((NR,)),
            dma((NC,)),
            dma((NR,)),
            pltpu.SemaphoreType.REGULAR,
            pltpu.SemaphoreType.REGULAR,
        ],
        compiler_params=pltpu.CompilerParams(
            collective_id=0, has_side_effects=True, vmem_limit_bytes=60 * 2**20
        ),
    )(
        pull_owner[:, 0], pull_slot, pull_target, nodes, weight, adjacency,
        history.reshape(8, BLK, HID), hist_tiles, cotangent,
    )
    all_nodes = nodes.shape[0] * NR * NC
    return pl.pallas_call(
        lambda *refs: finish(1.0 / math.sqrt(all_nodes), *refs),
        out_shape=(
            jax.ShapeDtypeStruct((SPAN, HID), BF16),
            jax.ShapeDtypeStruct((SPAN, HID), BF16),
            jax.ShapeDtypeStruct((HID, HID), F32),
        ),
        in_specs=[any_, any_, vmem],
        out_specs=(any_, any_, vmem),
        scratch_shapes=[dma((2,))],
    )(act, grad_nodes, gw.reshape(HID, HID))


def solution(mesh):
    return jax.shard_map(
        local,
        mesh=mesh,
        in_specs=(
            P(("row", "col"), None),
            P(),
            P("row", "col"),
            P(("row", "col"), None),
            P(("row", "col"), None),
            P(("row", "col")),
            P(("row", "col")),
            P(("row", "col"), None, None),
            P(("row", "col"), None),
        ),
        out_specs=(P(("row", "col"), None), P(("row", "col"), None), P()),
        check_vma=False,
    )
```

time: 146 us -> 115 us (0.79)
  Pallas kernels: 138 us -> 114 us
  local copies, waits for them, and re-layouts: 3.97 us -> 0 us
  other arithmetic: 2.97 us -> 0 us
    pallas_call x1, Pallas kernels: 138 us -> 103 us  [local(): pl.pallas_call(kernel, out_shape=(jax.ShapeDtypeStruct((SPAN, HID), BF16)...]
    pallas_call x0 -> x1, Pallas kernels: none -> 10.7 us  [local(): pl.pallas_call(lambda *refs: finish(1.0 / math.sqrt(all_nodes), *refs), o...]
    unnamed x2 -> x0, local copies, waits for them, and re-layouts: 3.13 us -> none
where the time goes in v2:
time: 115 us
  Pallas kernels  114 us (99%)
    pallas_call x1, Pallas kernels, local(): pl.pallas_call(kernel, out_shape=(jax.ShapeDtypeStruct((SPAN, HID), BF16)...  103 us
    pallas_call x1, Pallas kernels, local(): pl.pallas_call(lambda *refs: finish(1.0 / math.sqrt(all_nodes), *refs), o...  10.7 us

profile of v2, /device:TPU:1, one launch (start us, length us, event | category | flops | bytes accessed | tf_op | source)
XLA Modules:
  0.0 114.9 jit_solution(6260150942090210562)
XLA Ops:
  0.6 103.5 %shard_map.112 = (bf16[256,256]{1,0:T(8,128)(2,1)}, bf16[256,256]{1,0:T(8,128)(2,1)}, f32[16,16,256]{2,1,0:T(8,128)}) custom-call(s32[32]{0:T(128)} %bitcast.5, s32[32]{0:T(128)} %slot_ref.1, s32[32]{0:T(128)} %target_ref.1, bf16[256,256]{1,0:T(8,128)(2,1)} %nodes_hbm.1, bf16[256,256]{1,0:T(8,128)(2,1)} %w_hbm.1, bf16[2048,4096]{1,0:T(8,128)(2,1)} %adj_hbm.1, ...), custom_call_target="tpu_custom_call" | custom-call | tf_op jit(solution)/shard_map/pallas_call | solution.py:382
  104.1 10.7 %shard_map.113 = (bf16[256,256]{1,0:T(8,128)(2,1)}, bf16[256,256]{1,0:T(8,128)(2,1)}, f32[256,256]{1,0:T(8,128)}) custom-call(bf16[256,256]{1,0:T(8,128)(2,1)} %get-tuple-element.6.refs_0_, bf16[256,256]{1,0:T(8,128)(2,1)} %get-tuple-element.7.refs_1_, f32[256,256]{1,0:T(8,128)} %bitcast.4), custom_call_target="tpu_custom_call" | custom-call | tf_op jit(solution)/shard_map/pallas_call | solution.py:438

commit v3 on v2

--- a/solution.py
+++ b/solution.py
@@ -20,13 +20,13 @@
 
 
 def kernel(
-    owner_ref, slot_ref, target_ref, nodes_hbm, w_hbm, adj_hbm, hist_hbm, tiles_hbm, cot_hbm,
-    act_ref, gn_ref, gw_ref,
-    nodes_all, hist0, hist1, adj, w, cot, tiles, mix, inb, sums,
+    owner_hbm, slot_hbm, target_hbm, nodes_hbm, w_hbm, adj_hbm, hist_hbm, tiles_hbm, cot_hbm,
+    act_hbm, gn_hbm, gw_hbm,
+    owner_ref, slot_ref, target_ref, act_ref, gn_ref,
+    nodes_all, hist0, hist1, adj, w, cot, tiles, mix, mix_rcv, mix_snd, mix_far, mix_own, sums,
     rs_snd, rs_rcv, gt, sib_snd, sib_rcv, d_snd, d_rcv,
     gwt, gw_rcv1, gw_rcv2, gw_all, chain_v, chain_ref,
-    loc_sem, snd_sem, ag_sem, rs_sem, g_sem, sib_snd_sem, sib_sem, d_snd_sem, d_sem,
-    gw1_sem, gw2_sem, gw3_sem, near_sem, far_sem,
+    loc_sem, snd_sem, ag_sem, rs_sem, g_sem, sib_sem, d_sem, one_sem, near_sem, far_sem,
 ):
     r = lax.axis_index("row")
     c = lax.axis_index("col")
@@ -48,21 +48,26 @@
         return (xx * 4 + yy) * 2 + kk
 
     hist = (hist0, hist1)
-    sent = []
-
-    def send(src, dst, rsem, row, col):
-        copy = pltpu.make_async_remote_copy(
-            src_ref=src, dst_ref=dst, send_sem=snd_sem.at[len(sent)], recv_sem=rsem,
+    groups = dict(mixz=3, mixx=15, rs0=4, rs1=5, g0=6, g1=7, sib0=8, sib1=9, d0=10, d1=11, w1=12, w2=13, w3=14)
+    col_order = [
+        ((c // 4 + dx) % 2) * 4 + (z + dz) % 4
+        for dx, dz in ((1, 2), (0, 2), (1, 1), (0, 1), (1, 3), (0, 3), (1, 0))
+    ]
+
+    def copy_of(src, dst, group, rsem, row, col):
+        return pltpu.make_async_remote_copy(
+            src_ref=src, dst_ref=dst, send_sem=snd_sem.at[groups.get(group, group)], recv_sem=rsem,
             device_id=(row, col), device_id_type=MESH,
         )
-        copy.start()
-        sent.append(copy)
+
+    def send(src, dst, group, rsem, row, col):
+        copy_of(src, dst, group, rsem, row, col).start()
 
     def arrive(dst, rsem):
-        pltpu.make_async_remote_copy(
-            src_ref=dst, dst_ref=dst, send_sem=snd_sem.at[0], recv_sem=rsem,
-            device_id=(sib, c), device_id_type=MESH,
-        ).wait_recv()
+        copy_of(dst, dst, 0, rsem, sib, c).wait_recv()
+
+    def all_sent(src, group):
+        copy_of(src, src, group, one_sem.at[0], sib, c).wait_send()
 
     def local(src, dst, i):
         copy = pltpu.make_async_copy(src, dst, loc_sem.at[i])
@@ -81,6 +86,12 @@
     adj_copy = local(adj_hbm, adj, 4)
     tiles_copy = local(tiles_hbm, tiles, 5)
     cot_copy = local(cot_hbm, cot, 6)
+    pull_copies = [
+        local(src, dst, 8 + i)
+        for i, (src, dst) in enumerate(
+            ((target_hbm, target_ref), (owner_hbm, owner_ref), (slot_hbm, slot_ref))
+        )
+    ]
 
     barrier = pltpu.get_barrier_semaphore()
     for rr, cc in (
@@ -101,7 +112,7 @@
 
     def push(chunk, owner, part, dest):
         ref = piece(chunk, owner, part)
-        send(ref, ref, ag_sem.at[chunk, owner, part or 0], dest, c)
+        send(ref, ref, chunk, ag_sem.at[chunk, owner, part or 0], dest, c)
 
     def got(chunk, owner, part=None):
         arrive(piece(chunk, owner, part), ag_sem.at[chunk, owner, part or 0])
@@ -172,11 +183,35 @@
 
     def forward_piece(i):
         rows = pl.ds(i * 512, 512)
-        m = jnp.dot(adj[rows, :], nodes_all[...], preferred_element_type=F32).astype(BF16)
-        mix[rows, :] = m
-        v = jnp.dot(m, w[...], preferred_element_type=F32)
-        inb[0, rows, :] = v[:, :HALF]
-        inb[1, rows, :] = v[:, HALF:]
+        mix[rows, :] = jnp.dot(
+            adj[rows, :], nodes_all[...], preferred_element_type=F32
+        ).astype(BF16)
+
+    def scatter_mix():
+        for dz in (2, 1, 3):
+            zz = (z + dz) % 4
+            for xx in range(2):
+                send(
+                    mix.at[span(xx * 4 + zz)], mix_rcv.at[z, xx], "mixz", one_sem.at[0],
+                    r, c - z + zz,
+                )
+
+    def cross_mix():
+        arrive(mix_rcv.at[pl.ds(0, 3)], one_sem.at[0])
+        xx = c // 4
+        theirs = mix[span((1 - xx) * 4 + z), :].astype(F32)
+        for dz in range(1, 4):
+            theirs = theirs + mix_rcv[(z + dz) % 4, 1 - xx].astype(F32)
+        mix_snd[...] = theirs.astype(BF16)
+        send(mix_snd, mix_far, "mixx", one_sem.at[4], r, c_across)
+
+    def collect_mix():
+        xx = c // 4
+        total = mix[span(c), :].astype(F32)
+        for dz in range(1, 4):
+            total = total + mix_rcv[(z + dz) % 4, xx].astype(F32)
+        arrive(mix_far, one_sem.at[4])
+        mix_own[...] = (total + mix_far[...].astype(F32)).astype(BF16)
 
     def history_and_scatter(h):
         sums[0] = jnp.zeros((BLK, HALF), F32)
@@ -193,86 +228,79 @@
             return carry
 
         lax.fori_loop(0, K, link, 0, unroll=4)
-        for d in range(1, NC + 1):
-            cc = (c + d) % NC
+        for cc in col_order + [c]:
             for i in range(2):
-                j = cc * 2 + i
-                v = inb[h, pl.ds(pl.multiple_of(j * BLK, BLK), BLK), :] + sums[chain_ref[0, K + j]]
+                v = sums[chain_ref[0, K + cc * 2 + i]]
                 rs_snd[h, cc, pl.ds(i * BLK, BLK), :] = v.astype(BF16)
-            if d < NC:
-                send(rs_snd.at[h, cc], rs_rcv.at[h, c], rs_sem.at[h, c], r, cc)
+            if cc is not c:
+                send(rs_snd.at[h, cc], rs_rcv.at[h, c], f"rs{h}", rs_sem.at[h], r, cc)
 
     def activate(h):
         cols = pl.ds(h * HALF, HALF)
-        mixed = rs_snd[h, c].astype(F32)
-        for d in range(1, NC):
-            cc = (c + NC - d) % NC
-            arrive(rs_rcv.at[h, cc], rs_sem.at[h, cc])
+        mixed = jnp.dot(mix_own[...], w[:, cols], preferred_element_type=F32)
+        mixed = mixed + rs_snd[h, c].astype(F32)
+        arrive(rs_rcv.at[h, pl.ds(0, NC - 1)], rs_sem.at[h])
+        for cc in col_order:
             mixed = mixed + rs_rcv[h, cc].astype(F32)
         s = 1.0 / (1.0 + jnp.exp(-mixed))
         g = cot[:, cols].astype(F32) * s * (1.0 + mixed * (1.0 - s))
+        g = g.T.astype(BF16)
         own = gt.at[h, :, span(c)]
-        own[...] = g.T.astype(BF16)
-        for d in range(1, NC):
-            send(own, own, g_sem.at[h, c], r, (c + d) % NC)
+        own[...] = g
+        for cc in col_order:
+            send(own, own, f"g{h}", g_sem.at[h], r, cc)
+        gwt[pl.ds(h * HALF, HALF), :] = jnp.dot(g, mix_own[...], preferred_element_type=F32)
         act_ref[:, cols] = (mixed * s).astype(BF16)
 
+    def near(i):
+        return ((x + 1 - i % 2) % 2) * 4 + (y + 3 - i // 2) % 4
+
     def sib_copy(h, q):
-        return pltpu.make_async_remote_copy(
-            src_ref=sib_snd.at[h, q], dst_ref=sib_rcv.at[h, q], send_sem=sib_snd_sem.at[h, q],
-            recv_sem=sib_sem.at[h, q], device_id=(sib, c), device_id_type=MESH,
+        return copy_of(sib_snd.at[h, q], sib_rcv.at[h, q], f"sib{h}", sib_sem.at[h, q], sib, c)
+
+    def row_copy(h, q):
+        return copy_of(
+            d_snd.at[h, q], d_rcv.at[h, chip], f"d{h}", d_sem.at[h], q * 2 + core, c
         )
 
-    def row_copy(h, q):
-        return pltpu.make_async_remote_copy(
-            src_ref=d_snd.at[h, q], dst_ref=d_rcv.at[h, chip], send_sem=d_snd_sem.at[h, q],
-            recv_sem=d_sem.at[h, chip], device_id=(q * 2 + core, c), device_id_type=MESH,
-        )
-
     def backward(h):
-        for d in range(1, NC):
-            cc = (c + NC - d) % NC
-            arrive(gt.at[h, :, span(cc)], g_sem.at[h, cc])
-        gwt[pl.ds(h * HALF, HALF), :] = jnp.dot(gt[h], mix[...], preferred_element_type=F32)
-        if h:
-            for d in range(1, NR):
-                rr = (r + d) % NR
-                rows = pl.ds(pl.multiple_of(rr * 16, 16), 16)
-                send(gwt.at[rows], gw_rcv1.at[r], gw1_sem.at[r], rr, c)
-
-        def for_sib(d, carry):
-            q = (chip + d) % 8
+        arrive(gt.at[h, :, pl.ds(0, (NC - 1) * SPAN)], g_sem.at[h])
+
+        def for_sib(i, carry):
+            q = near(i)
             v = jnp.dot(gt[h], adj[:, span(2 * q + 1 - core)], preferred_element_type=F32)
             sib_snd[h, q] = v.astype(BF16)
             sib_copy(h, q).start()
             return carry
 
-        lax.fori_loop(1, 9, for_sib, 0)
+        lax.fori_loop(0, 8, for_sib, 0)
 
         def summed(q):
             v = jnp.dot(gt[h], adj[:, span(2 * q + core)], preferred_element_type=F32)
             arrive(sib_rcv.at[h, q], sib_sem.at[h, q])
             d_snd[h, q] = (v + sib_rcv[h, q].astype(F32)).astype(BF16)
 
-        def for_chip(d, carry):
-            q = (chip + d) % 8
+        def for_chip(i, carry):
+            q = near(i)
             summed(q)
             row_copy(h, q).start()
             return carry
 
-        lax.fori_loop(1, 8, for_chip, 0)
+        lax.fori_loop(0, 7, for_chip, 0)
         summed(chip)
 
     def collect_rows(h):
+        arrive(d_rcv.at[h, pl.ds(0, 7)], d_sem.at[h])
         total = d_snd[h, chip].astype(F32)
         for d in range(1, 8):
-            qq = (chip + 8 - d) % 8
-            arrive(d_rcv.at[h, qq], d_sem.at[h, qq])
-            total = total + d_rcv[h, qq].astype(F32)
+            total = total + d_rcv[h, (chip + d) % 8].astype(F32)
         return lax.dot_general(
             total.T.astype(BF16), w[:, pl.ds(h * HALF, HALF)], (((1,), (1,)), ((), ())),
             preferred_element_type=F32,
         )
+
+    def weight_rows(i):
+        return pl.ds(pl.multiple_of(i * 16, 16), 16)
 
     own_nodes.wait()
     own_y(0)
@@ -283,6 +311,8 @@
     for cc in (z_up, z_down):
         pl.semaphore_signal(near_sem, inc=1, device_id=(r, cc), device_id_type=MESH)
     own_hist[1].wait()
+    for copy in pull_copies:
+        copy.wait()
     chain_copy = make_chain()
     step_b(0)
     step_a(0)
@@ -303,6 +333,8 @@
     step_d(1)
     forward_piece(2)
     forward_piece(3)
+    pl.semaphore_wait(far_sem, 1)
+    scatter_mix()
     step_b(2)
     step_a(2)
     step_e(1)
@@ -310,72 +342,67 @@
     tiles_copy.wait()
     cot_copy.wait()
     chain_copy.wait()
-    pl.semaphore_wait(far_sem, 1)
     step_f(1)
     history_and_scatter(0)
     step_d(2)
     step_c(2)
-    activate(0)
+    cross_mix()
     step_e(2)
     step_f(2)
     history_and_scatter(1)
+    collect_mix()
+    activate(0)
+    activate(1)
+    act_copy = local(act_ref, act_hbm, 11)
+    for d in range(1, NR):
+        rr = (r + d) % NR
+        send(gwt.at[weight_rows(rr)], gw_rcv1.at[r], "w1", one_sem.at[1], rr, c)
     backward(0)
-    activate(1)
-    part = collect_rows(0)
+    arrive(gw_rcv1.at[pl.ds(0, NR - 1)], one_sem.at[1])
+    total = gwt[weight_rows(r), :]
+    for d in range(1, NR):
+        total = total + gw_rcv1[(r + d) % NR]
+    gw_rcv2[c] = total
+    for cc in col_order:
+        send(gw_rcv2.at[c], gw_rcv2.at[c], "w2", one_sem.at[2], r, cc)
     backward(1)
-    total = gwt[pl.ds(pl.multiple_of(r * 16, 16), 16), :]
-    for d in range(1, NR):
-        rr = (r + NR - d) % NR
-        arrive(gw_rcv1.at[rr], gw1_sem.at[rr])
-        total = total + gw_rcv1[rr]
-    gw_rcv2[c] = total
-    for d in range(1, NC):
-        send(gw_rcv2.at[c], gw_rcv2.at[c], gw2_sem.at[c], r, (c + d) % NC)
-    for d in range(1, NC):
-        cc = (c + NC - d) % NC
-        arrive(gw_rcv2.at[cc], gw2_sem.at[cc])
+    arrive(gw_rcv2.at[pl.ds(0, NC - 1)], one_sem.at[2])
     total = gw_rcv2[0]
     for i in range(1, NC):
         total = total + gw_rcv2[i]
     gw_all[r] = total
     for d in range(1, NR):
-        send(gw_all.at[r], gw_all.at[r], gw3_sem.at[r], (r + d) % NR, c)
+        send(gw_all.at[r], gw_all.at[r], "w3", one_sem.at[3], (r + d) % NR, c)
+    part = collect_rows(0)
     gn_ref[...] = (part + collect_rows(1)).astype(BF16)
-    for d in range(1, NR):
-        rr = (r + NR - d) % NR
-        arrive(gw_all.at[rr], gw3_sem.at[rr])
-    gw_ref[...] = gw_all[...]
-    for copy in sent:
-        copy.wait_send()
-
-    def sent_tiles(d, carry):
-        q = (chip + d) % 8
-        for h in range(2):
-            sib_copy(h, q).wait_send()
-            row_copy(h, q).wait_send()
-        return carry
-
-    lax.fori_loop(1, 8, sent_tiles, 0)
+    gn_copy = local(gn_ref, gn_hbm, 12)
+    arrive(gw_all.at[pl.ds(0, NR - 1)], one_sem.at[3])
+    gw_copy = local(gw_all, gw_hbm, 13)
+    all_sent(nodes_all.at[pl.ds(0, 15 * SPAN)], 0)
     for h in range(2):
-        sib_copy(h, chip).wait_send()
-
-
-def finish(scale, act_ref, gn_ref, gw_ref, act_out, gn_out, gw_out, sem):
-    copies = [
-        pltpu.make_async_copy(act_ref, act_out, sem.at[0]),
-        pltpu.make_async_copy(gn_ref, gn_out, sem.at[1]),
-    ]
-    for copy in copies:
-        copy.start()
+        all_sent(hist[h].at[pl.ds(0, 120)], 1 + h)
+        all_sent(rs_snd.at[h, pl.ds(0, NC - 1)], f"rs{h}")
+        all_sent(gt.at[h, :, pl.ds(0, (NC - 1) * SPAN)], f"g{h}")
+        all_sent(sib_snd.at[h], f"sib{h}")
+        all_sent(d_snd.at[h, pl.ds(0, 7)], f"d{h}")
+    all_sent(mix.at[pl.ds(0, 6 * SPAN)], "mixz")
+    all_sent(mix_snd, "mixx")
+    all_sent(gwt.at[pl.ds(0, (NR - 1) * 16)], "w1")
+    all_sent(gw_rcv2.at[pl.ds(0, NC - 1)], "w2")
+    all_sent(gw_all.at[pl.ds(0, NR - 1)], "w3")
+    for copy in (act_copy, gn_copy, gw_copy):
+        copy.wait()
+
+
+def finish(scale, act_ref, gn_ref, gw_ref, act_out, gn_out, gw_out):
+    act_out[...] = act_ref[...]
+    gn_out[...] = gn_ref[...]
     gw_out[...] = gw_ref[...].T * scale
-    for copy in copies:
-        copy.wait()
 
 
 def local(
     nodes, weight, adjacency, history, pull_owner, pull_slot, pull_target, hist_tiles, cotangent
 ):
-    smem = pl.BlockSpec(memory_space=pltpu.SMEM)
     any_ = pl.BlockSpec(memory_space=pl.ANY)
     vmem = pl.BlockSpec(memory_space=pltpu.VMEM)
     dma = pltpu.SemaphoreType.DMA
@@ -386,9 +413,14 @@
             jax.ShapeDtypeStruct((SPAN, HID), BF16),
             jax.ShapeDtypeStruct((NR, 16, HID), F32),
         ),
-        in_specs=[smem] * 3 + [any_] * 6,
-        out_specs=(vmem,) * 3,
+        in_specs=[any_] * 9,
+        out_specs=(any_,) * 3,
         scratch_shapes=[
+            pltpu.SMEM((K,), jnp.int32),
+            pltpu.SMEM((K,), jnp.int32),
+            pltpu.SMEM((K,), jnp.int32),
+            pltpu.VMEM((SPAN, HID), BF16),
+            pltpu.VMEM((SPAN, HID), BF16),
             pltpu.VMEM((4096, HID), BF16),
             pltpu.VMEM((128, BLK, HALF), BF16),
             pltpu.VMEM((128, BLK, HALF), BF16),
@@ -397,7 +429,10 @@
             pltpu.VMEM((SPAN, HID), BF16),
             pltpu.VMEM((K, BLK, BLK), BF16),
             pltpu.VMEM((2048, HID), BF16),
-            pltpu.VMEM((2, 2048, HALF), F32),
+            pltpu.VMEM((4, 2, SPAN, HID), BF16),
+            pltpu.VMEM((SPAN, HID), BF16),
+            pltpu.VMEM((SPAN, HID), BF16),
+            pltpu.VMEM((SPAN, HID), BF16),
             pltpu.VMEM((K + 1, BLK, HALF), F32),
             pltpu.VMEM((2, NC, SPAN, HALF), BF16),
             pltpu.VMEM((2, NC, SPAN, HALF), BF16),
@@ -412,18 +447,14 @@
             pltpu.VMEM((NR, 16, HID), F32),
             pltpu.VMEM((1, 128), jnp.int32),
             pltpu.SMEM((1, 128), jnp.int32),
-            dma((8,)),
-            dma((160,)),
+            dma((14,)),
+            dma((16,)),
             dma((3, NR, 2)),
-            dma((2, NC)),
-            dma((2, NC)),
+            dma((2,)),
+            dma((2,)),
             dma((2, 8)),
-            dma((2, 8)),
-            dma((2, 8)),
-            dma((2, 8)),
-            dma((NR,)),
-            dma((NC,)),
-            dma((NR,)),
+            dma((2,)),
+            dma((5,)),
             pltpu.SemaphoreType.REGULAR,
             pltpu.SemaphoreType.REGULAR,
         ],
@@ -442,9 +473,8 @@
             jax.ShapeDtypeStruct((SPAN, HID), BF16),
             jax.ShapeDtypeStruct((HID, HID), F32),
         ),
-        in_specs=[any_, any_, vmem],
-        out_specs=(any_, any_, vmem),
-        scratch_shapes=[dma((2,))],
+        in_specs=[vmem] * 3,
+        out_specs=(vmem,) * 3,
     )(act, grad_nodes, gw.reshape(HID, HID))
 
 

time: 115 us -> 99 us (0.86)
  Pallas kernels: 114 us -> 98.2 us
    pallas_call x1, Pallas kernels: 10.7 us -> 1.92 us  [local(): pl.pallas_call(lambda *refs: finish(1.0 / math.sqrt(all_nodes), *refs), o...]
    pallas_call x1, Pallas kernels: 103 us -> 96.3 us  [local(): pl.pallas_call(kernel, out_shape=(jax.ShapeDtypeStruct((SPAN, HID), BF16)...]
where the time goes in v3:
time: 99 us; the launch traced here: 98.9 us
  Pallas kernels  98.2 us (99%)
    pallas_call x1, Pallas kernels, local(): pl.pallas_call(kernel, out_shape=(jax.ShapeDtypeStruct((SPAN, HID), BF16)...  96.3 us

profile of v3, /device:TPU:1, one launch (start us, length us, event | category | flops | bytes accessed | tf_op | source)
XLA Modules:
  0.0 98.9 jit_solution(14340233627082066795)
XLA Ops:
  0.6 96.3 %shard_map.112 = (bf16[256,256]{1,0:T(8,128)(2,1)}, bf16[256,256]{1,0:T(8,128)(2,1)}, f32[16,16,256]{2,1,0:T(8,128)}) custom-call(s32[32]{0:T(128)} %bitcast.5, s32[32]{0:T(128)} %slot_hbm.1, s32[32]{0:T(128)} %target_hbm.1, bf16[256,256]{1,0:T(8,128)(2,1)} %nodes_hbm.1, bf16[256,256]{1,0:T(8,128)(2,1)} %w_hbm.1, bf16[2048,4096]{1,0:T(8,128)(2,1)} %adj_hbm.1, ...), custom_call_target="tpu_custom_call" | custom-call | tf_op jit(solution)/shard_map/pallas_call | solution.py:409
  96.9 1.9 %shard_map.113 = (bf16[256,256]{1,0:T(8,128)(2,1)}, bf16[256,256]{1,0:T(8,128)(2,1)}, f32[256,256]{1,0:T(8,128)}) custom-call(bf16[256,256]{1,0:T(8,128)(2,1)} %get-tuple-element.6.refs_0_, bf16[256,256]{1,0:T(8,128)(2,1)} %get-tuple-element.7.refs_1_, f32[256,256]{1,0:T(8,128)} %bitcast.4), custom_call_target="tpu_custom_call" | custom-call | tf_op jit(solution)/shard_map/pallas_call | solution.py:469

commit v4 on v3

--- a/solution.py
+++ b/solution.py
@@ -25,7 +25,7 @@
     owner_ref, slot_ref, target_ref, act_ref, gn_ref,
     nodes_all, hist0, hist1, adj, w, cot, tiles, mix, mix_rcv, mix_snd, mix_far, mix_own, sums,
     rs_snd, rs_rcv, gt, sib_snd, sib_rcv, d_snd, d_rcv,
-    gwt, gw_rcv1, gw_rcv2, gw_all, chain_v, chain_ref,
+    gwt, gwt_snd, gw_rcv1, gw_rcv2, gw_all, chain_v, chain_ref,
     loc_sem, snd_sem, ag_sem, rs_sem, g_sem, sib_sem, d_sem, one_sem, near_sem, far_sem,
 ):
     r = lax.axis_index("row")
@@ -249,7 +249,9 @@
         own[...] = g
         for cc in col_order:
             send(own, own, f"g{h}", g_sem.at[h], r, cc)
-        gwt[pl.ds(h * HALF, HALF), :] = jnp.dot(g, mix_own[...], preferred_element_type=F32)
+        term = jnp.dot(g, mix_own[...], preferred_element_type=F32)
+        gwt[pl.ds(h * HALF, HALF), :] = term
+        gwt_snd[pl.ds(h * HALF, HALF), :] = term.astype(BF16)
         act_ref[:, cols] = (mixed * s).astype(BF16)
 
     def near(i):
@@ -356,21 +358,21 @@
     act_copy = local(act_ref, act_hbm, 11)
     for d in range(1, NR):
         rr = (r + d) % NR
-        send(gwt.at[weight_rows(rr)], gw_rcv1.at[r], "w1", one_sem.at[1], rr, c)
+        send(gwt_snd.at[weight_rows(rr)], gw_rcv1.at[r], "w1", one_sem.at[1], rr, c)
     backward(0)
     arrive(gw_rcv1.at[pl.ds(0, NR - 1)], one_sem.at[1])
     total = gwt[weight_rows(r), :]
     for d in range(1, NR):
-        total = total + gw_rcv1[(r + d) % NR]
-    gw_rcv2[c] = total
+        total = total + gw_rcv1[(r + d) % NR].astype(F32)
+    gw_rcv2[c] = total.astype(BF16)
     for cc in col_order:
         send(gw_rcv2.at[c], gw_rcv2.at[c], "w2", one_sem.at[2], r, cc)
     backward(1)
     arrive(gw_rcv2.at[pl.ds(0, NC - 1)], one_sem.at[2])
-    total = gw_rcv2[0]
+    total = gw_rcv2[0].astype(F32)
     for i in range(1, NC):
-        total = total + gw_rcv2[i]
-    gw_all[r] = total
+        total = total + gw_rcv2[i].astype(F32)
+    gw_all[r] = total.astype(BF16)
     for d in range(1, NR):
         send(gw_all.at[r], gw_all.at[r], "w3", one_sem.at[3], (r + d) % NR, c)
     part = collect_rows(0)
@@ -387,7 +389,7 @@
         all_sent(d_snd.at[h, pl.ds(0, 7)], f"d{h}")
     all_sent(mix.at[pl.ds(0, 6 * SPAN)], "mixz")
     all_sent(mix_snd, "mixx")
-    all_sent(gwt.at[pl.ds(0, (NR - 1) * 16)], "w1")
+    all_sent(gwt_snd.at[pl.ds(0, (NR - 1) * 16)], "w1")
     all_sent(gw_rcv2.at[pl.ds(0, NC - 1)], "w2")
     all_sent(gw_all.at[pl.ds(0, NR - 1)], "w3")
     for copy in (act_copy, gn_copy, gw_copy):
@@ -397,7 +399,7 @@
 def finish(scale, act_ref, gn_ref, gw_ref, act_out, gn_out, gw_out):
     act_out[...] = act_ref[...]
     gn_out[...] = gn_ref[...]
-    gw_out[...] = gw_ref[...].T * scale
+    gw_out[...] = gw_ref[...].astype(F32).T * scale
 
 
 def local(
@@ -411,7 +413,7 @@
         out_shape=(
             jax.ShapeDtypeStruct((SPAN, HID), BF16),
             jax.ShapeDtypeStruct((SPAN, HID), BF16),
-            jax.ShapeDtypeStruct((NR, 16, HID), F32),
+            jax.ShapeDtypeStruct((NR, 16, HID), BF16),
         ),
         in_specs=[any_] * 9,
         out_specs=(any_,) * 3,
@@ -442,9 +444,10 @@
             pltpu.VMEM((2, 8, HALF, SPAN), BF16),
             pltpu.VMEM((2, 8, HALF, SPAN), BF16),
             pltpu.VMEM((HID, HID), F32),
-            pltpu.VMEM((NR, 16, HID), F32),
-            pltpu.VMEM((NC, 16, HID), F32),
-            pltpu.VMEM((NR, 16, HID), F32),
+            pltpu.VMEM((HID, HID), BF16),
+            pltpu.VMEM((NR, 16, HID), BF16),
+            pltpu.VMEM((NC, 16, HID), BF16),
+            pltpu.VMEM((NR, 16, HID), BF16),
             pltpu.VMEM((1, 128), jnp.int32),
             pltpu.SMEM((1, 128), jnp.int32),
             dma((14,)),

time: 99 us -> 97.4 us (0.984)
  Pallas kernels: 98.2 us -> 96.7 us
    pallas_call x1, Pallas kernels: 96.3 us -> 94.8 us  [local(): pl.pallas_call(kernel, out_shape=(jax.ShapeDtypeStruct((SPAN, HID), BF16)...]
where the time goes in v4:
time: 97.4 us; the launch traced here: 97.3 us
  Pallas kernels  96.7 us (99%)
    pallas_call x1, Pallas kernels, local(): pl.pallas_call(kernel, out_shape=(jax.ShapeDtypeStruct((SPAN, HID), BF16)...  94.8 us

profile of v4, /device:TPU:1, one launch (start us, length us, event | category | flops | bytes accessed | tf_op | source)
XLA Modules:
  0.0 97.3 jit_solution(14832384652152551504)
XLA Ops:
  0.6 94.8 %shard_map.112 = (bf16[256,256]{1,0:T(8,128)(2,1)}, bf16[256,256]{1,0:T(8,128)(2,1)}, bf16[16,16,256]{2,1,0:T(8,128)(2,1)}) custom-call(s32[32]{0:T(128)} %bitcast.5, s32[32]{0:T(128)} %slot_hbm.1, s32[32]{0:T(128)} %target_hbm.1, bf16[256,256]{1,0:T(8,128)(2,1)} %nodes_hbm.1, bf16[256,256]{1,0:T(8,128)(2,1)} %w_hbm.1, bf16[2048,4096]{1,0:T(8,128)(2,1)} %adj_hbm.1, ...), custom_call_target="tpu_custom_call" | custom-call | tf_op jit(solution)/shard_map/pallas_call | solution.py:411
  95.5 1.8 %shard_map.113 = (bf16[256,256]{1,0:T(8,128)(2,1)}, bf16[256,256]{1,0:T(8,128)(2,1)}, f32[256,256]{1,0:T(8,128)}) custom-call(bf16[256,256]{1,0:T(8,128)(2,1)} %get-tuple-element.6.refs_0_, bf16[256,256]{1,0:T(8,128)(2,1)} %get-tuple-element.7.refs_1_, bf16[256,256]{1,0:T(8,128)(2,1)} %bitcast.4), custom_call_target="tpu_custom_call" | custom-call | tf_op jit(solution)/shard_map/pallas_call | solution.py:472

commit v5 on v4

--- a/solution.py
+++ b/solution.py
@@ -54,6 +54,13 @@
         for dx, dz in ((1, 2), (0, 2), (1, 1), (0, 1), (1, 3), (0, 3), (1, 0))
     ]
 
+    row_order = [
+        row_of((x + dx) % 2, (y + dy) % 4, (core + dk) % 2)
+        for dx, dy in ((1, 2), (0, 2), (1, 1), (0, 1), (1, 3), (0, 3), (1, 0), (0, 0))
+        for dk in range(2)
+        if dx or dy or dk
+    ]
+
     def copy_of(src, dst, group, rsem, row, col):
         return pltpu.make_async_remote_copy(
             src_ref=src, dst_ref=dst, send_sem=snd_sem.at[groups.get(group, group)], recv_sem=rsem,
@@ -221,13 +228,13 @@
             sums[k + 1] = jnp.dot(tiles[k], block, preferred_element_type=F32)
             return carry
 
-        lax.fori_loop(0, K, product, 0, unroll=8)
+        lax.fori_loop(0, K, product, 0, unroll=16)
 
         def link(k, carry):
             sums[k + 1] = sums[k + 1] + sums[chain_ref[0, k]]
             return carry
 
-        lax.fori_loop(0, K, link, 0, unroll=4)
+        lax.fori_loop(0, K, link, 0, unroll=8)
         for cc in col_order + [c]:
             for i in range(2):
                 v = sums[chain_ref[0, K + cc * 2 + i]]
@@ -356,8 +363,7 @@
     activate(0)
     activate(1)
     act_copy = local(act_ref, act_hbm, 11)
-    for d in range(1, NR):
-        rr = (r + d) % NR
+    for rr in row_order:
         send(gwt_snd.at[weight_rows(rr)], gw_rcv1.at[r], "w1", one_sem.at[1], rr, c)
     backward(0)
     arrive(gw_rcv1.at[pl.ds(0, NR - 1)], one_sem.at[1])
@@ -373,8 +379,8 @@
     for i in range(1, NC):
         total = total + gw_rcv2[i].astype(F32)
     gw_all[r] = total.astype(BF16)
-    for d in range(1, NR):
-        send(gw_all.at[r], gw_all.at[r], "w3", one_sem.at[3], (r + d) % NR, c)
+    for rr in row_order:
+        send(gw_all.at[r], gw_all.at[r], "w3", one_sem.at[3], rr, c)
     part = collect_rows(0)
     gn_ref[...] = (part + collect_rows(1)).astype(BF16)
     gn_copy = local(gn_ref, gn_hbm, 12)

time: 97.4 us -> 96.8 us (level)
  no operation moved by 1% of the time
where the time goes in v5:
time: 96.8 us; the launch traced here: 96.6 us
  Pallas kernels  96 us (99%)
    pallas_call x1, Pallas kernels, local(): pl.pallas_call(kernel, out_shape=(jax.ShapeDtypeStruct((SPAN, HID), BF16)...  94.1 us

profile of v5, /device:TPU:1, one launch (start us, length us, event | category | flops | bytes accessed | tf_op | source)
XLA Modules:
  0.0 96.6 jit_solution(4927266244784751333)
XLA Ops:
  0.6 94.1 %shard_map.112 = (bf16[256,256]{1,0:T(8,128)(2,1)}, bf16[256,256]{1,0:T(8,128)(2,1)}, bf16[16,16,256]{2,1,0:T(8,128)(2,1)}) custom-call(s32[32]{0:T(128)} %bitcast.5, s32[32]{0:T(128)} %slot_hbm.1, s32[32]{0:T(128)} %target_hbm.1, bf16[256,256]{1,0:T(8,128)(2,1)} %nodes_hbm.1, bf16[256,256]{1,0:T(8,128)(2,1)} %w_hbm.1, bf16[2048,4096]{1,0:T(8,128)(2,1)} %adj_hbm.1, ...), custom_call_target="tpu_custom_call" | custom-call | tf_op jit(solution)/shard_map/pallas_call | solution.py:417
  94.8 1.8 %shard_map.113 = (bf16[256,256]{1,0:T(8,128)(2,1)}, bf16[256,256]{1,0:T(8,128)(2,1)}, f32[256,256]{1,0:T(8,128)}) custom-call(bf16[256,256]{1,0:T(8,128)(2,1)} %get-tuple-element.6.refs_0_, bf16[256,256]{1,0:T(8,128)(2,1)} %get-tuple-element.7.refs_1_, bf16[256,256]{1,0:T(8,128)(2,1)} %bitcast.4), custom_call_target="tpu_custom_call" | custom-call | tf_op jit(solution)/shard_map/pallas_call | solution.py:478
